TPU v7x, 128 devices: a whole 4x4x4 slice. The times are simulated.
128 devices in a mesh: ctx: 16 (over z, x_lo, core), tp: 8 (over y, x_hi).
Axes of the slice: x: 4 (x_hi: 2, x_lo: 2; x = x_hi * 2 + x_lo), y: 4, z: 4, core: 2. Of those that a mesh axis runs over, the one named last changes fastest.
Arguments:
- projected: bfloat16 [3, 4096, 8192], P(None, 'ctx', 'tp'), may hold values from -6 to 6
- short_taps: float32 [3, 7, 8192], P(None, None, 'tp'), may hold values from -2.4 to 2.4
- range_filter: bfloat16 [64, 1024], P('tp'), may hold values from -0.1875 to 0.1875
- skip_gain: float32 [8192], P('tp'), may hold values from -4 to 4
- out_weight: bfloat16 [8192, 8192], P('ctx', 'tp'), may hold values from -0.0625 to 0.0625
Outputs:
- mixed: bfloat16 [4096, 8192], P('ctx', 'tp')
All inputs are finite; a program needn't handle non-finite values.
Results may differ from a plain program's by a relative error of at most 0.0057.
Values may be sent and summed in bfloat16 or wider, within the bound.
A program may use at most 192 MiB of HBM per device.

v0:
```python
import jax
import jax.numpy as jnp
from jax import lax
from jax.sharding import PartitionSpec as P


def passed_along(block, axis, distance):
    devices = range(lax.axis_size(axis))
    route = [((i - distance) % len(devices), i) for i in devices]
    return lax.ppermute(block, axis, route)


def short_conv(extended, tap_rows, length):
    accumulated = jnp.zeros((length, extended.shape[1]), jnp.float32)
    rim_width = tap_rows.shape[0] - 1
    for lag_index in range(tap_rows.shape[0]):
        window = extended[rim_width - lag_index : rim_width - lag_index + length]
        accumulated = accumulated + tap_rows[lag_index][None, :] * window.astype(jnp.float32)
    return accumulated


def toeplitz_slabs(range_filter, length, span_blocks):
    kept = range_filter.shape[1]
    offsets = lax.broadcasted_iota(jnp.int32, (span_blocks + 1, length, length), 0)
    rows_at = lax.broadcasted_iota(jnp.int32, (span_blocks + 1, length, length), 1)
    cols_at = lax.broadcasted_iota(jnp.int32, (span_blocks + 1, length, length), 2)
    lag_at = offsets * length + rows_at - cols_at
    inside = jnp.logical_and(lag_at >= 0, lag_at < kept)
    clipped = jnp.clip(lag_at, 0, kept - 1)
    looked = jnp.take(range_filter, clipped.reshape(-1), axis=1).reshape(
        range_filter.shape[0], span_blocks + 1, length, length
    )
    return jnp.where(inside[None], looked, jnp.zeros((), range_filter.dtype))


def local(projected, short_taps, range_filter, skip_gain, out_weight):
    length = projected.shape[1]
    width_dev = projected.shape[2]
    groups = range_filter.shape[0]
    group_width = width_dev // groups
    rim_width = short_taps.shape[1] - 1
    span_blocks = range_filter.shape[1] // length
    rim_block = passed_along(projected[:, length - rim_width :, :], "ctx", 1)
    extended = jnp.concatenate([rim_block, projected], axis=1)
    query_feat = short_conv(extended[0], short_taps[0], length)
    key_feat = short_conv(extended[1], short_taps[1], length)
    value_feat = short_conv(extended[2], short_taps[2], length)
    mixed_in = (key_feat * value_feat).astype(jnp.bfloat16)
    slabs = toeplitz_slabs(range_filter, length, span_blocks)

    def correlate(arrived, offset):
        grouped = arrived.reshape(length, groups, group_width)
        product = jnp.einsum(
            "gam,mgc->agc", slabs[:, offset], grouped, preferred_element_type=jnp.float32
        )
        return product.reshape(length, width_dev)

    toeplitz = correlate(mixed_in, 0)
    for offset in range(1, span_blocks + 1):
        arrived = passed_along(mixed_in, "ctx", offset)
        toeplitz = toeplitz + correlate(arrived, offset)
    restored = lax.optimization_barrier(mixed_in).astype(jnp.float32)
    gated_out = (query_feat * (toeplitz + skip_gain[None, :] * restored)).astype(jnp.bfloat16)
    gathered = lax.all_gather(gated_out, "tp", axis=1, tiled=True)
    summed = jnp.dot(
        gathered,
        lax.all_gather(out_weight, "ctx", axis=0, tiled=True),
        preferred_element_type=jnp.float32,
    )
    return summed.astype(jnp.bfloat16)


def solution(mesh):
    placed = (P(None, "ctx", "tp"), P(None, None, "tp"), P("tp", None), P("tp"), P("ctx", "tp"))
    return jax.shard_map(
        local, mesh=mesh, in_specs=placed, out_specs=P("ctx", "tp"), check_vma=False
    )
```

profile of v0, /device:TPU:1, one launch (start us, length us, event | category | flops | bytes accessed | tf_op | source)
XLA Modules:
  0.0 1476.2 jit_solution(5024653289956213897)
XLA Ops:
  6.5 1.5 slice.240
  8.0 2.6 collective-permute-start
  15.7 1133.3 %gather_fusion = bf16[327680,8]{1,0:T(8,128)(2,1)} fusion(bf16[8,1024]{0,1:T(8,128)(2,1)S(1)} %copy.40, s32[327680]{0:T(1024)S(1)} %broadcast_clamp_fusion), kind=kCustom, calls=%fused_computation | custom fusion | bytes 11796480 | tf_op jit(solution)/shard_map/jit(_take)/gather | solution.py:30
  1149.1 60.1 %copy.42 = bf16[8,5,256,256]{3,2,0,1:T(8,128)(2,1)} copy(bf16[8,5,256,256]{0,3,2,1:T(8,128)(2,1)} %bitcast.44) | data formatting | bytes 10485760 | tf_op jit(solution)/shard_map/jit(_take)/gather | solution.py:30
  1209.2 6.1 select_select_fusion
  1216.3 3.8 fusion.19
  1220.1 1.7 collective-permute-start.4
  1222.5 2.4 collective-permute-start.1
  1227.5 3.4 fusion.58
  1230.9 2.5 copy.60
  1233.5 2.5 copy.59
  1236.0 2.5 copy.58
  1238.6 2.6 copy.57
  1242.4 3.9 fusion.46
  1246.4 2.6 copy.55
  1249.0 2.5 copy.54
  1251.5 2.5 copy.53
  1254.0 2.5 copy.52
  1256.6 2.6 copy.51
  1259.2 2.5 copy.50
  1263.0 2.6 copy.48
  1265.7 7.1 fusion.8
  1275.1 2.9 fusion.6
  1278.0 2.1 copy.43
  1280.0 2.7 fusion.7
  1282.7 2.7 convolution_add_fusion.1
  1286.8 3.3 fusion.1
  1290.2 1.6 copy.47
  1291.8 3.0 fusion.11
  1295.6 69.1 %all-gather.3.cloned.1.call-done = bf16[256,8192]{1,0:T(8,128)(2,1)} async-done(((bf16[256,1024]{1,0:T(8,128)(2,1)}), bf16[256,8192]{1,0:T(8,128)(2,1)}) %all-gather.3.cloned.1.call-update) | async-done | bytes 4194320 | tf_op jit(solution)/shard_map/all_gather | solution.py:64
  1364.7 92.4 %all-gather.5.cloned.1.call-done = bf16[8192,1024]{1,0:T(8,128)(2,1)} async-done(((bf16[512,1024]{1,0:T(8,128)(2,1)}), bf16[8192,1024]{1,0:T(8,128)(2,1)}) %all-gather.5.cloned.1.call-update) | async-done | bytes 16777232 | tf_op jit(solution)/shard_map/all_gather | solution.py:67
  1457.1 12.3 convolution_convert_fusion
  (84 shorter events, 16.4 us)
Async XLA Ops:
  6.5 5.4 copy-start.3
  6.5 6.1 copy-start.20
  6.5 1358.2 %all-gather.3.cloned.1.call-start = ((), (), s32[]{:S(2)}) async-start(), calls=%async_computation | async-start | bytes 4718592 | tf_op jit(solution)/shard_map/all_gather | solution.py:64
  8.0 1208.2 %collective-permute-start = (bf16[3,6,1024]{2,1,0:T(8,128)(2,1)}, bf16[3,6,1024]{2,1,0:T(8,128)(2,1)}, u32[]{:S(2)}, u32[]{:S(2)}) collective-permute-start(bf16[3,6,1024]{2,1,0:T(8,128)(2,1)} %slice.240), channel_id=1, source_target_pairs={{120,0},{0,8},{8,16},{16,24},{24,32},{32,40},{40,48},{48,56},{56,6... | collective-permute-start | bytes 110600 | tf_op jit(solution)/shard_map/ppermute | solution.py:10
  1209.1 7.1 copy-start
  1209.2 7.1 copy-start.4
  1209.2 7.1 copy-start.6
  1209.2 7.1 copy-start.8
  1209.2 7.1 copy-start.10
  1209.2 7.1 copy-start.12
  1209.2 7.1 copy-start.14
  1209.2 7.1 copy-start.16
  1209.2 7.1 copy-start.18
  1220.1 52.7 %collective-permute-start.4 = (bf16[256,1024]{1,0:T(8,128)(2,1)}, bf16[256,1024]{1,0:T(8,128)(2,1)S(1)}, u32[]{:S(2)}, u32[]{:S(2)}) collective-permute-start(bf16[256,1024]{1,0:T(8,128)(2,1)} %get-tuple-element.5), channel_id=1, source_target_pairs={{96,0},{104,8},{112,16},{120,24},{0,32},{8,40},{16,48},{24,56},{32... | collective-permute-start | bytes 1572872 | tf_op jit(solution)/shard_map/ppermute | solution.py:10
  1221.8 52.0 %collective-permute-start.3 = (bf16[256,1024]{1,0:T(8,128)(2,1)}, bf16[256,1024]{1,0:T(8,128)(2,1)}, u32[]{:S(2)}, u32[]{:S(2)}) collective-permute-start(bf16[256,1024]{1,0:T(8,128)(2,1)} %get-tuple-element.5), channel_id=1, source_target_pairs={{104,0},{112,8},{120,16},{0,24},{8,32},{16,40},{24,48},{32,56},{40... | collective-permute-start | bytes 1572872 | tf_op jit(solution)/shard_map/ppermute | solution.py:10
  1222.5 55.4 %collective-permute-start.1 = (bf16[256,1024]{1,0:T(8,128)(2,1)}, bf16[256,1024]{1,0:T(8,128)(2,1)}, u32[]{:S(2)}, u32[]{:S(2)}) collective-permute-start(bf16[256,1024]{1,0:T(8,128)(2,1)} %get-tuple-element.5), channel_id=1, source_target_pairs={{120,0},{0,8},{8,16},{16,24},{24,32},{32,40},{40,48},{48,56},{56,6... | collective-permute-start | bytes 1572872 | tf_op jit(solution)/shard_map/ppermute | solution.py:10
  1224.9 60.5 %collective-permute-start.2 = (bf16[256,1024]{1,0:T(8,128)(2,1)}, bf16[256,1024]{1,0:T(8,128)(2,1)}, u32[]{:S(2)}, u32[]{:S(2)}) collective-permute-start(bf16[256,1024]{1,0:T(8,128)(2,1)} %get-tuple-element.5), channel_id=1, source_target_pairs={{112,0},{120,8},{0,16},{8,24},{16,32},{24,40},{32,48},{40,56},{48,... | collective-permute-start | bytes 1572872 | tf_op jit(solution)/shard_map/ppermute | solution.py:10
  1261.7 3.9 copy-start.5
  1261.7 3.9 copy-start.7
  1261.7 3.9 copy-start.9
  1261.7 3.9 copy-start.11
  1261.7 3.9 copy-start.13
  1261.7 3.9 copy-start.15
  1261.7 3.9 copy-start.17
  1261.7 3.9 copy-start.19
  1280.0 2.7 copy-start.2
  1290.2 1.6 copy-start.24
  1290.2 1.7 copy-start.25
  1290.2 1.7 copy-start.26
  1290.2 1.7 copy-start.27
  1290.2 1.7 copy-start.28
  1294.8 162.2 %all-gather.5.cloned.1.call-start = ((), (), s32[]{:S(2)}) async-start(), calls=%async_computation.1 | async-start | bytes 17825792 | tf_op jit(solution)/shard_map/all_gather | solution.py:67
  (4 other events, 6.3 us)
Sparse Core Ops, SparseCore 0:
  1295.0 69.6 all-gather.2
  1366.4 90.6 all-gather.4
where the time goes:
time: 1480 us
  local copies, waits for them, and re-layouts  1240 us (84%)
  waiting for transfers between devices  162 us (11%)
  matrix products  31.1 us (2%)
  other arithmetic  23.1 us (2%)
    gather x2, local copies, waits for them, and re-layouts, toeplitz_slabs(): jnp.take(range_filter, clipped.reshape(-1), axis=1)  1190 us
    all_gather x1, waiting for transfers between devices, local(): lax.all_gather(out_weight, 'ctx', axis=0, tiled=True)  92.4 us
    all_gather x1, waiting for transfers between devices, local(): gathered = lax.all_gather(gated_out, 'tp', axis=1, tiled=True)  69.1 us
    convert_element_type x14, local copies, waits for them, and re-layouts, short_conv(): window.astype(jnp.float32)  32 us
  transfers between devices with their start and end apart: 7, of which 2 were waited for; matrix products, arithmetic and copies ran while one was open for 86% of the time, Pallas kernels for 0%

commit v1 on v0

--- a/solution.py
+++ b/solution.py
@@ -61,7 +61,9 @@
         toeplitz = toeplitz + correlate(arrived, offset)
     restored = lax.optimization_barrier(mixed_in).astype(jnp.float32)
     gated_out = (query_feat * (toeplitz + skip_gain[None, :] * restored)).astype(jnp.bfloat16)
-    gathered = lax.all_gather(gated_out, "tp", axis=1, tiled=True)
+    gathered = jnp.concatenate(
+        lax.all_to_all(jnp.stack([gated_out] * lax.axis_size("tp")), "tp", 0, 0), axis=1
+    )
     summed = jnp.dot(
         gathered,
         lax.all_gather(out_weight, "ctx", axis=0, tiled=True),

time: 1480 us -> 1370 us (0.926)
  waiting for transfers between devices: 162 us -> 0.03 us
  blocking collectives: 0 us -> 57.3 us
    all_gather x1, waiting for transfers between devices: 92.4 us -> 0.01 us  [local(): lax.all_gather(out_weight, 'ctx', axis=0, tiled=True)]
    all_gather x1 -> x0, waiting for transfers between devices: 69.1 us -> none  [local(): gathered = lax.all_gather(gated_out, 'tp', axis=1, tiled=True)]
    all_to_all x0 -> x1, blocking collectives: none -> 57.3 us  [local(): lax.all_to_all(jnp.stack([gated_out] * lax.axis_size('tp')), 'tp', 0, 0)]
  transfers between devices with their start and end apart: 7 -> 6, of which waited for: 2 -> 0; matrix products, arithmetic and copies ran while one was open for 86% -> 93% of each run, Pallas kernels for 0% -> 0%
where the time goes in v1:
time: 1370 us
  local copies, waits for them, and re-layouts  1250 us (91%)
  blocking collectives  57.3 us (4%)
  matrix products  27.4 us (2%)
  other arithmetic  19.2 us (1%)
    gather x2, local copies, waits for them, and re-layouts, toeplitz_slabs(): jnp.take(range_filter, clipped.reshape(-1), axis=1)  1200 us
    all_to_all x1, blocking collectives, local(): lax.all_to_all(jnp.stack([gated_out] * lax.axis_size('tp')), 'tp', 0, 0)  57.3 us
    convert_element_type x14, local copies, waits for them, and re-layouts, short_conv(): window.astype(jnp.float32)  32.2 us
  transfers between devices with their start and end apart: 6, of which 0 were waited for; matrix products, arithmetic and copies ran while one was open for 93% of the time, Pallas kernels for 0%

profile of v1, /device:TPU:1, one launch (start us, length us, event | category | flops | bytes accessed | tf_op | source)
XLA Modules:
  0.0 1371.7 jit_solution(13394615820131813043)
XLA Ops:
  7.4 2.7 collective-permute-start
  13.5 1141.3 %gather_fusion = bf16[327680,8]{1,0:T(8,128)(2,1)} fusion(bf16[8,1024]{0,1:T(8,128)(2,1)S(1)} %copy.40, s32[327680]{0:T(1024)S(1)} %broadcast_clamp_fusion), kind=kCustom, calls=%fused_computation | custom fusion | bytes 11796480 | tf_op jit(solution)/shard_map/jit(_take)/gather | solution.py:30
  1154.9 60.1 %copy.42 = bf16[8,5,256,256]{3,2,0,1:T(8,128)(2,1)} copy(bf16[8,5,256,256]{0,3,2,1:T(8,128)(2,1)} %bitcast.44) | data formatting | bytes 10485760 | tf_op jit(solution)/shard_map/jit(_take)/gather | solution.py:30
  1216.0 6.1 select_select_fusion
  1222.1 2.7 fusion.19
  1224.8 1.6 collective-permute-start.4
  1227.2 2.4 collective-permute-start.1
  1232.2 2.5 fusion.58
  1234.7 2.5 copy.61
  1237.2 2.6 copy.60
  1239.8 2.5 copy.59
  1242.3 2.6 copy.58
  1246.2 3.0 fusion.46
  1249.2 2.6 copy.56
  1251.8 2.6 copy.55
  1254.4 2.6 copy.54
  1257.0 2.5 copy.53
  1259.5 2.6 copy.52
  1262.1 2.6 copy.51
  1266.0 2.6 copy.49
  1268.5 7.1 fusion.8
  1276.9 2.0 copy.45
  1278.9 2.0 copy.43
  1281.0 2.1 copy.44
  1283.0 1.8 fusion.6
  1284.8 1.8 fusion.7
  1286.6 1.8 convolution_add_fusion.1
  1288.4 2.7 fusion.1
  1291.1 1.6 copy.47
  1292.7 2.1 fusion.11
  1295.3 57.3 %all_to_all.5 = bf16[8,256,1024]{1,2,0:T(8,128)(2,1)} all-to-all(bf16[8,256,1024]{1,2,0:T(8,128)(2,1)S(1)} %stack.2), channel_id=1, replica_groups=mesh['ctx'=16,'tp'=8] {'tp'}, dimensions={0} | all-to-all | bytes 8388608 | tf_op jit(solution)/shard_map/all_to_all | solution.py:65
  1352.5 12.4 convolution_convert_fusion
  (40 shorter events, 13.1 us)
Async XLA Ops:
  6.5 1346.0 %all-gather.2.cloned.1.call-start = ((), (), s32[]{:S(2)}) async-start(), calls=%async_computation.1 | async-start | bytes 17825792 | tf_op jit(solution)/shard_map/all_gather | solution.py:69
  7.4 1214.8 %collective-permute-start = (bf16[3,6,1024]{2,1,0:T(8,128)(2,1)S(1)}, bf16[3,6,1024]{2,1,0:T(8,128)(2,1)S(1)}, u32[]{:S(2)}, u32[]{:S(2)}) collective-permute-start(bf16[3,6,1024]{2,1,0:T(8,128)(2,1)S(1)} %slice.240), channel_id=1, source_target_pairs={{120,0},{0,8},{8,16},{16,24},{24,32},{32,40},{40,48},{48,56},{56,6... | collective-permute-start | bytes 110600 | tf_op jit(solution)/shard_map/ppermute | solution.py:10
  11.7 1.4 copy-start.5
  1154.9 60.1 %copy-start.4 = (f32[3,7,1024]{2,1,0:T(8,128)S(1)}, f32[3,7,1024]{2,1,0:T(8,128)}, u32[]{:S(2)}) copy-start(f32[3,7,1024]{2,1,0:T(8,128)} %param.6) | copy-start | bytes 258052
  1216.0 6.1 copy-start
  1224.8 50.8 %collective-permute-start.4 = (bf16[256,1024]{1,0:T(8,128)(2,1)}, bf16[256,1024]{1,0:T(8,128)(2,1)}, u32[]{:S(2)}, u32[]{:S(2)}) collective-permute-start(bf16[256,1024]{1,0:T(8,128)(2,1)} %get-tuple-element.5), channel_id=1, source_target_pairs={{96,0},{104,8},{112,16},{120,24},{0,32},{8,40},{16,48},{24,56},{32... | collective-permute-start | bytes 1572872 | tf_op jit(solution)/shard_map/ppermute | solution.py:10
  1226.5 50.4 %collective-permute-start.3 = (bf16[256,1024]{1,0:T(8,128)(2,1)}, bf16[256,1024]{1,0:T(8,128)(2,1)}, u32[]{:S(2)}, u32[]{:S(2)}) collective-permute-start(bf16[256,1024]{1,0:T(8,128)(2,1)} %get-tuple-element.5), channel_id=1, source_target_pairs={{104,0},{112,8},{120,16},{0,24},{8,32},{16,40},{24,48},{32,56},{40... | collective-permute-start | bytes 1572872 | tf_op jit(solution)/shard_map/ppermute | solution.py:10
  1227.2 51.7 %collective-permute-start.1 = (bf16[256,1024]{1,0:T(8,128)(2,1)}, bf16[256,1024]{1,0:T(8,128)(2,1)}, u32[]{:S(2)}, u32[]{:S(2)}) collective-permute-start(bf16[256,1024]{1,0:T(8,128)(2,1)} %get-tuple-element.5), channel_id=1, source_target_pairs={{120,0},{0,8},{8,16},{16,24},{24,32},{32,40},{40,48},{48,56},{56,6... | collective-permute-start | bytes 1572872 | tf_op jit(solution)/shard_map/ppermute | solution.py:10
  1229.6 51.4 %collective-permute-start.2 = (bf16[256,1024]{1,0:T(8,128)(2,1)}, bf16[256,1024]{1,0:T(8,128)(2,1)}, u32[]{:S(2)}, u32[]{:S(2)}) collective-permute-start(bf16[256,1024]{1,0:T(8,128)(2,1)} %get-tuple-element.5), channel_id=1, source_target_pairs={{112,0},{120,8},{0,16},{8,24},{16,32},{24,40},{32,48},{40,56},{48,... | collective-permute-start | bytes 1572872 | tf_op jit(solution)/shard_map/ppermute | solution.py:10
  1283.0 1.8 copy-start.1
  1284.8 1.8 copy-start.2
  1286.6 1.8 copy-start.3
  1291.1 1.6 copy-start.6
Sparse Core Ops, SparseCore 0:
  10.2 94.0 all-gather.1
